TPU v7x, 256 devices: a whole 4x4x8 slice. The times are simulated.
256 devices in a mesh: node: 64 (over z, y, core), state: 4 (over x).
Axes of the slice: x: 4, y: 4, z: 8, core: 2. Of those that a mesh axis runs over, the one named last changes fastest.
Arguments:
- block: bfloat16 [64, 2097152], P('state', 'node'), may hold values from -6 to 6
- connectivity: int32 [125, 32768], P(None, 'node'), may hold values from 0 to 49151, as said below
- potential: float32 [125, 32768], P(None, 'node'), may hold values from 0.1 to 3
- cell_matrix: bfloat16 [125, 125], replicated, as said below
Outputs:
- orthonormal: bfloat16 [64, 2097152], P('state', 'node')
- factor: float32 [64, 64], replicated
Inputs may be any that keep to these rules, and one draw needn't show every extreme that they name: `connectivity`: in each slab, numbers below 8192 are the previous slab's last 8192 nodes and numbers from 40960 on are the next slab's first nodes. The numbers of the slab's k-th cell (k from 0) lie in k * 96 to k * 96 + 2 * 96 - 1, those of its last cell in k * 96 to k * 96 + 95; each cell reaches the lower end of its range. `cell_matrix`: Symmetric.
All inputs are finite; a program needn't handle non-finite values.
Results may differ from a plain program's by a relative error of at most 0.015.
Values may be sent and summed in bfloat16 or wider, within the bound.
No kernel may reach another device: no remote copies, remote signals or barrier semaphores. Data moves between devices by JAX's collectives and lax.ppermute only.
A program may use at most 64 MiB of HBM per device.

v0:
```python
import jax
import jax.numpy as jnp
from jax import lax
from jax.sharding import PartitionSpec as P

CENTER = 3.0
HALF_WIDTH = 3.0


def extended(block, sides, width):
    for axis, dim in sides:
        count = lax.axis_size(axis)
        forward = [(i, i + 1) for i in range(count - 1)]
        backward = [(target, source) for source, target in forward]
        low = lax.ppermute(
            lax.slice_in_dim(block, block.shape[dim] - width, None, axis=dim), axis, forward
        )
        high = lax.ppermute(lax.slice_in_dim(block, 0, width, axis=dim), axis, backward)
        block = jnp.concatenate([low, block, high], axis=dim)
    return block


def passed_along(block, axis, distance):
    devices = range(lax.axis_size(axis))
    route = [(i - distance, i) for i in devices if i - distance in devices]
    return lax.ppermute(block, axis, route)


def cell_terms(window, connectivity, potential, cell_matrix):
    states = window.shape[0]
    cells = connectivity.shape[1]
    stride = window.shape[1] // cells
    segments = window.reshape(states, cells, stride)
    following = jnp.concatenate(
        [segments[:, 1:], jnp.zeros((states, 1, stride), segments.dtype)], axis=1
    )
    paired = jnp.concatenate([segments, following], axis=2)
    offsets = jnp.arange(cells, dtype=jnp.int32) * stride
    local_links = connectivity - offsets[None, :]
    columns = jnp.arange(2 * stride, dtype=jnp.int32)
    group = min(cells, 128)
    pieces = []
    for first_cell in range(0, cells, group):
        links = local_links[:, first_cell : first_cell + group]
        picker = links[:, :, None] == columns[None, None, :]
        picker_half = picker.astype(jnp.bfloat16)
        part_pair = paired[:, first_cell : first_cell + group]
        values = jnp.einsum(
            "skn,jkn->sjk", part_pair, picker_half, preferred_element_type=jnp.float32
        )
        mixed = jnp.einsum(
            "ij,sjk->sik",
            cell_matrix,
            values.astype(jnp.bfloat16),
            preferred_element_type=jnp.float32,
        )
        mixed = mixed + potential[None, :, first_cell : first_cell + group] * values
        spread = jnp.einsum(
            "sjk,jkn->skn", mixed, picker.astype(jnp.float32), precision=lax.Precision.HIGHEST
        )
        pieces.append(spread)
    spread = jnp.concatenate(pieces, axis=1)
    lower = spread[:, :, :stride]
    upper = spread[:, :, stride:]
    shifted = jnp.concatenate([jnp.zeros((states, 1, stride), jnp.float32), upper[:, :-1]], axis=1)
    return (lower + shifted).reshape(states, cells * stride)


def operate(field, connectivity, potential, cell_matrix):
    owned = field.shape[1]
    margin = owned // 4
    window = extended(field, (("node", 1),), margin)
    summed = cell_terms(window, connectivity, potential, cell_matrix)
    result = summed[:, margin : margin + owned]
    from_above = passed_along(summed[:, :margin].astype(jnp.bfloat16), "node", -1).astype(
        jnp.float32
    )
    from_below = passed_along(summed[:, margin + owned :].astype(jnp.bfloat16), "node", 1).astype(
        jnp.float32
    )
    result = result.at[:, owned - margin :].add(from_above)
    result = result.at[:, :margin].add(from_below)
    return result


def factorize(intersection):
    factor = jnp.linalg.cholesky(intersection)
    identity = jnp.eye(intersection.shape[0], dtype=factor.dtype)
    inverse = lax.linalg.triangular_solve(factor, identity, left_side=True, lower=True).astype(
        jnp.bfloat16
    )
    return (factor, inverse)


def per_device(block, connectivity, potential, cell_matrix):
    start = block.astype(jnp.float32)
    image = operate(block, connectivity, potential, cell_matrix)
    first = ((image - CENTER * start) / HALF_WIDTH).astype(jnp.bfloat16)
    image = operate(first, connectivity, potential, cell_matrix)
    second = (2.0 * (image - CENTER * first.astype(jnp.float32)) / HALF_WIDTH - start).astype(
        jnp.bfloat16
    )
    total_nodes = block.shape[1] * lax.axis_size("node")
    panel = lax.all_gather(second, "state", axis=0, tiled=True)
    partial_intersection = jnp.einsum("an,bn->ab", panel, panel, preferred_element_type=jnp.float32)
    intersection = lax.psum(partial_intersection, "node") / total_nodes
    factor, inverse = factorize(intersection)
    rows = second.shape[0]
    mine = lax.dynamic_slice_in_dim(inverse, lax.axis_index("state") * rows, rows, 0)
    orthonormal = jnp.dot(mine, panel, preferred_element_type=jnp.float32).astype(jnp.bfloat16)
    return (orthonormal, factor)


def solution(mesh):
    return jax.shard_map(
        per_device,
        mesh=mesh,
        in_specs=(P("state", "node"), P(None, "node"), P(None, "node"), P()),
        out_specs=(P("state", "node"), P()),
        check_vma=False,
    )
```

profile of v0, /device:TPU:2, one launch (start us, length us, event | category | flops | bytes accessed | tf_op | source)
XLA Modules:
  0.0 566.9 jit_solution(16091128970053678684)
XLA Ops:
  28.4 4.3 fusion.122
  33.6 4.3 fusion.121
  39.8 4.2 fusion.120
  45.8 11.6 %fusion.42 = f32[16,128,192]{2,0,1:T(8,128)S(1)} fusion(s32[125,128]{0,1:T(8,128)S(1)} %copy.16, f32[16,128,125]{2,0,1:T(8,128)S(1)} %copy.33, f32[16,125,128]{1,0,2:T(8,128)} %get-tuple-element.75, f32[125,128]{0,1:T(8,128)} %copy.19), kind=kOutput, calls=%fused_computation.59 | convolution fusion | flops 593408000 | bytes 3748864 | tf_op jit(solution)/shard_map/sjk,jkn->skn/dot_general | solution.py:58
  57.4 9.9 %fusion.44 = f32[16,128,192]{2,0,1:T(8,128)S(1)} fusion(s32[125,128]{0,1:T(8,128)S(1)} %copy-done.11, f32[16,128,125]{2,0,1:T(8,128)S(1)} %copy.35, f32[16,125,128]{1,0,2:T(8,128)S(1)} %copy-done.19, f32[125,128]{0,1:T(8,128)S(1)} %copy-done.14), kind=kOutput, calls=%fused_computation.61 | convolution fusion | flops 593408000 | bytes 3748864 | tf_op jit(solution)/shard_map/sjk,jkn->skn/dot_general | solution.py:58
  67.3 10.0 %fusion.46 = f32[16,128,192]{2,0,1:T(8,128)S(1)} fusion(s32[125,128]{0,1:T(8,128)S(1)} %copy.22, f32[16,128,125]{2,0,1:T(8,128)S(1)} %copy-done.7, f32[16,125,128]{1,0,2:T(8,128)S(1)} %copy-done.20, f32[125,128]{0,1:T(8,128)S(1)} %copy.23), kind=kOutput, calls=%fused_computation.63 | convolution fusion | flops 593408000 | bytes 3748864 | tf_op jit(solution)/shard_map/sjk,jkn->skn/dot_general | solution.py:58
  77.3 9.8 %fusion.48 = f32[16,128,192]{2,0,1:T(8,128)S(1)} fusion(s32[125,128]{0,1:T(8,128)S(1)} %copy.24, f32[16,128,125]{2,0,1:T(8,128)S(1)} %copy-done.9, f32[16,125,128]{1,0,2:T(8,128)S(1)} %copy-done.21, f32[125,128]{0,1:T(8,128)S(1)} %copy.25), kind=kOutput, calls=%fused_computation.65 | convolution fusion | flops 593408000 | bytes 3748864 | tf_op jit(solution)/shard_map/sjk,jkn->skn/dot_general | solution.py:58
  90.5 3.2 copy.26
  93.8 4.0 reshape.133
  100.0 6.8 %collective-permute-start.3 = (bf16[16,8192]{1,0:T(8,128)(2,1)S(1)}, bf16[16,8192]{1,0:T(8,128)(2,1)S(1)}, u32[]{:S(2)}, u32[]{:S(2)}) collective-permute-start(bf16[16,8192]{1,0:T(8,128)(2,1)S(1)} %get-tuple-element.54), channel_id=1, source_target_pairs={{0,4},{4,8},{8,12},{12,16},{16,20},{20,24},{24,28},{28,32},{32,36}... | collective-permute-start | bytes 786440 | tf_op jit(solution)/shard_map/ppermute | solution.py:26
  109.2 5.8 %collective-permute-start.4 = (bf16[16,8192]{1,0:T(8,128)(2,1)S(1)}, bf16[16,8192]{1,0:T(8,128)(2,1)S(1)}, u32[]{:S(2)}, u32[]{:S(2)}) collective-permute-start(bf16[16,8192]{1,0:T(8,128)(2,1)S(1)} %get-tuple-element.56), channel_id=1, source_target_pairs={{0,4},{4,8},{8,12},{12,16},{16,20},{20,24},{24,28},{28,32},{32,36}... | collective-permute-start | bytes 786440 | tf_op jit(solution)/shard_map/ppermute | solution.py:15
  116.3 4.1 collective-permute-done.5
  147.0 11.7 %fusion.43 = f32[16,128,192]{2,0,1:T(8,128)S(1)} fusion(s32[125,128]{0,1:T(8,128)S(1)} %copy.16, f32[16,128,125]{2,0,1:T(8,128)} %copy.41, f32[16,125,128]{1,0,2:T(8,128)} %get-tuple-element.83, f32[125,128]{0,1:T(8,128)} %copy.19), kind=kOutput, calls=%fused_computation.60 | convolution fusion | flops 593408000 | bytes 3748864 | tf_op jit(solution)/shard_map/sjk,jkn->skn/dot_general | solution.py:58
  158.8 9.9 %fusion.45 = f32[16,128,192]{2,0,1:T(8,128)S(1)} fusion(s32[125,128]{0,1:T(8,128)S(1)} %copy-done.13, f32[16,128,125]{2,0,1:T(8,128)S(1)} %copy-done.8, f32[16,125,128]{1,0,2:T(8,128)S(1)} %copy-done.18, f32[125,128]{0,1:T(8,128)S(1)} %copy-done.15), kind=kOutput, calls=%fused_computation.62 | convolution fusion | flops 593408000 | bytes 3748864 | tf_op jit(solution)/shard_map/sjk,jkn->skn/dot_general | solution.py:58
  168.7 10.0 %fusion.47 = f32[16,128,192]{2,0,1:T(8,128)S(1)} fusion(s32[125,128]{0,1:T(8,128)S(1)} %copy.22, f32[16,128,125]{2,0,1:T(8,128)S(1)} %copy.45, f32[16,125,128]{1,0,2:T(8,128)S(1)} %copy-done.17, f32[125,128]{0,1:T(8,128)S(1)} %copy.23), kind=kOutput, calls=%fused_computation.64 | convolution fusion | flops 593408000 | bytes 3748864 | tf_op jit(solution)/shard_map/sjk,jkn->skn/dot_general | solution.py:58
  178.7 9.8 %fusion.49 = f32[16,128,192]{2,0,1:T(8,128)S(1)} fusion(s32[125,128]{0,1:T(8,128)S(1)} %copy.24, f32[16,128,125]{2,0,1:T(8,128)S(1)} %copy.47, f32[16,125,128]{1,0,2:T(8,128)S(1)} %copy-done.16, f32[125,128]{0,1:T(8,128)S(1)} %copy.25), kind=kOutput, calls=%fused_computation.66 | convolution fusion | flops 593408000 | bytes 3748864 | tf_op jit(solution)/shard_map/sjk,jkn->skn/dot_general | solution.py:58
  195.2 4.0 reshape.135
  201.0 7.3 %collective-permute-start.7 = (bf16[16,8192]{1,0:T(8,128)(2,1)S(1)}, bf16[16,8192]{1,0:T(8,128)(2,1)S(1)}, u32[]{:S(2)}, u32[]{:S(2)}) collective-permute-start(bf16[16,8192]{1,0:T(8,128)(2,1)S(1)} %get-tuple-element.52), channel_id=1, source_target_pairs={{0,4},{4,8},{8,12},{12,16},{16,20},{20,24},{24,28},{28,32},{32,36}... | collective-permute-start | bytes 786440 | tf_op jit(solution)/shard_map/ppermute | solution.py:26
  211.7 75.3 %all-gather.2.cloned.1.call-done = bf16[64,32768]{1,0:T(8,128)(2,1)} async-done(((bf16[16,32768]{1,0:T(8,128)(2,1)}), bf16[64,32768]{1,0:T(8,128)(2,1)}) %all-gather.2.cloned.1.call-update) | async-done | bytes 4194320 | tf_op jit(solution)/shard_map/all_gather | solution.py:104
  287.0 4.7 fusion.128
  291.7 251.0 %psum.7 = f32[64,64]{0,1:T(8,128)S(1)} all-reduce(f32[64,64]{0,1:T(8,128)S(1)} %fusion.128), channel_id=1, replica_groups=mesh['node'=64,'state'=4] {'node'}, use_global_device_ids=true, to_apply=%region_1.0 | all-reduce | flops 4096 | bytes 32768 | tf_op jit(solution)/shard_map/psum | solution.py:106
  542.8 5.8 %cholesky.17 = f32[64,64]{1,0:T(8,128)S(1)} custom-call(f32[64,64]{1,0:T(8,128)S(1)} %fusion.104), custom_call_target="Cholesky" | custom-call | tf_op jit(solution)/shard_map/jit(cholesky)/cholesky | solution.py:87
  550.6 4.9 custom-call.6
  555.8 3.8 convolution_convert_fusion
  (128 shorter events, 75.3 us)
Async XLA Ops:
  7.2 20.4 %copy-start = (bf16[125,125]{1,0:T(8,128)(2,1)S(1)}, bf16[125,125]{1,0:T(8,128)(2,1)}, u32[]{:S(2)}) copy-start(bf16[125,125]{1,0:T(8,128)(2,1)} %param.15) | copy-start | bytes 93754
  7.2 279.8 %all-gather.2.cloned.1.call-start = ((), (), s32[]{:S(2)}) async-start(), calls=%async_computation | async-start | bytes 5242880 | tf_op jit(solution)/shard_map/all_gather | solution.py:104
  8.4 7.1 %collective-permute-start = (bf16[16,8192]{1,0:T(8,128)(2,1)S(1)}, bf16[16,8192]{1,0:T(8,128)(2,1)S(1)}, u32[]{:S(2)}, u32[]{:S(2)}) collective-permute-start(bf16[16,8192]{1,0:T(8,128)(2,1)S(1)} %get-tuple-element.58), channel_id=1, source_target_pairs={{0,4},{4,8},{8,12},{12,16},{16,20},{20,24},{24,28},{28,32},{32,36}... | collective-permute-start | bytes 786440 | tf_op jit(solution)/shard_map/ppermute | solution.py:15
  10.1 5.4 collective-permute-start.1
  14.4 14.1 %copy-start.10 = (s32[125,128]{0,1:T(8,128)}, s32[125,128]{0,1:T(8,128)S(1)}, u32[]{:S(2)}) copy-start(s32[125,128]{0,1:T(8,128)S(1)} %copy.20) | copy-start | bytes 192004
  45.8 11.6 %copy-start.11 = (s32[125,128]{0,1:T(8,128)S(1)}, s32[125,128]{0,1:T(8,128)}, u32[]{:S(2)}) copy-start(s32[125,128]{0,1:T(8,128)} %copy-done.10) | copy-start | bytes 192004
  45.8 11.6 %copy-start.14 = (f32[125,128]{0,1:T(8,128)S(1)}, f32[125,128]{0,1:T(8,128)}, u32[]{:S(2)}) copy-start(f32[125,128]{0,1:T(8,128)} %copy.21) | copy-start | bytes 192004
  45.8 11.6 %copy-start.19 = (f32[16,125,128]{1,0,2:T(8,128)S(1)}, f32[16,125,128]{1,0,2:T(8,128)}, u32[]{:S(2)}) copy-start(f32[16,125,128]{1,0,2:T(8,128)} %get-tuple-element.73) | copy-start | bytes 3072004
  67.3 10.0 %copy-start.9 = (f32[16,128,125]{2,0,1:T(8,128)S(1)}, f32[16,128,125]{2,0,1:T(8,128)}, u32[]{:S(2)}) copy-start(f32[16,128,125]{2,0,1:T(8,128)} %copy.39) | copy-start | bytes 3072004
  67.3 10.0 %copy-start.21 = (f32[16,125,128]{1,0,2:T(8,128)S(1)}, f32[16,125,128]{1,0,2:T(8,128)}, u32[]{:S(2)}) copy-start(f32[16,125,128]{1,0,2:T(8,128)} %get-tuple-element.69) | copy-start | bytes 3072004
  98.0 8.9 %collective-permute-start.2 = (bf16[16,8192]{1,0:T(8,128)(2,1)S(1)}, bf16[16,8192]{1,0:T(8,128)(2,1)S(1)}, u32[]{:S(2)}, u32[]{:S(2)}) collective-permute-start(bf16[16,8192]{1,0:T(8,128)(2,1)S(1)} %get-tuple-element.55), channel_id=1, source_target_pairs={{4,0},{8,4},{12,8},{16,12},{20,16},{24,20},{28,24},{32,28},{36,32}... | collective-permute-start | bytes 786440 | tf_op jit(solution)/shard_map/ppermute | solution.py:26
  100.0 8.0 %collective-permute-start.3 = (bf16[16,8192]{1,0:T(8,128)(2,1)S(1)}, bf16[16,8192]{1,0:T(8,128)(2,1)S(1)}, u32[]{:S(2)}, u32[]{:S(2)}) collective-permute-start(bf16[16,8192]{1,0:T(8,128)(2,1)S(1)} %get-tuple-element.54), channel_id=1, source_target_pairs={{0,4},{4,8},{8,12},{12,16},{16,20},{20,24},{24,28},{28,32},{32,36}... | collective-permute-start | bytes 786440 | tf_op jit(solution)/shard_map/ppermute | solution.py:26
  109.2 11.3 %copy-start.4 = (bf16[16,32768]{1,0:T(8,128)(2,1)}, bf16[16,32768]{1,0:T(8,128)(2,1)S(1)}, u32[]{:S(2)}) copy-start(bf16[16,32768]{1,0:T(8,128)(2,1)S(1)} %fusion.40) | copy-start | bytes 3145732
  109.2 7.1 %collective-permute-start.4 = (bf16[16,8192]{1,0:T(8,128)(2,1)S(1)}, bf16[16,8192]{1,0:T(8,128)(2,1)S(1)}, u32[]{:S(2)}, u32[]{:S(2)}) collective-permute-start(bf16[16,8192]{1,0:T(8,128)(2,1)S(1)} %get-tuple-element.56), channel_id=1, source_target_pairs={{0,4},{4,8},{8,12},{12,16},{16,20},{20,24},{24,28},{28,32},{32,36}... | collective-permute-start | bytes 786440 | tf_op jit(solution)/shard_map/ppermute | solution.py:15
  115.0 5.4 collective-permute-start.5
  147.0 11.7 %copy-start.8 = (f32[16,128,125]{2,0,1:T(8,128)S(1)}, f32[16,128,125]{2,0,1:T(8,128)}, u32[]{:S(2)}) copy-start(f32[16,128,125]{2,0,1:T(8,128)} %copy.43) | copy-start | bytes 3072004
  147.0 11.7 %copy-start.13 = (s32[125,128]{0,1:T(8,128)S(1)}, s32[125,128]{0,1:T(8,128)}, u32[]{:S(2)}) copy-start(s32[125,128]{0,1:T(8,128)} %copy-done.10) | copy-start | bytes 192004
  147.0 11.7 %copy-start.15 = (f32[125,128]{0,1:T(8,128)S(1)}, f32[125,128]{0,1:T(8,128)}, u32[]{:S(2)}) copy-start(f32[125,128]{0,1:T(8,128)} %copy.21) | copy-start | bytes 192004
  147.0 11.7 %copy-start.18 = (f32[16,125,128]{1,0,2:T(8,128)S(1)}, f32[16,125,128]{1,0,2:T(8,128)}, u32[]{:S(2)}) copy-start(f32[16,125,128]{1,0,2:T(8,128)} %get-tuple-element.81) | copy-start | bytes 3072004
  168.6 10.1 %copy-start.16 = (f32[16,125,128]{1,0,2:T(8,128)S(1)}, f32[16,125,128]{1,0,2:T(8,128)}, u32[]{:S(2)}) copy-start(f32[16,125,128]{1,0,2:T(8,128)} %get-tuple-element.77) | copy-start | bytes 3072004
  199.4 10.9 %copy-start.3 = (bf16[16,32768]{1,0:T(8,128)(2,1)S(1)}, bf16[16,32768]{1,0:T(8,128)(2,1)}, u32[]{:S(2)}) copy-start(bf16[16,32768]{1,0:T(8,128)(2,1)} %param.12) | copy-start | bytes 3145732
  199.4 10.9 %copy-start.5 = (bf16[16,32768]{1,0:T(8,128)(2,1)S(1)}, bf16[16,32768]{1,0:T(8,128)(2,1)}, u32[]{:S(2)}) copy-start(bf16[16,32768]{1,0:T(8,128)(2,1)} %copy-done.4) | copy-start | bytes 3145732
  199.4 8.9 %collective-permute-start.6 = (bf16[16,8192]{1,0:T(8,128)(2,1)S(1)}, bf16[16,8192]{1,0:T(8,128)(2,1)S(1)}, u32[]{:S(2)}, u32[]{:S(2)}) collective-permute-start(bf16[16,8192]{1,0:T(8,128)(2,1)S(1)} %get-tuple-element.53), channel_id=1, source_target_pairs={{4,0},{8,4},{12,8},{16,12},{20,16},{24,20},{28,24},{32,28},{36,32}... | collective-permute-start | bytes 786440 | tf_op jit(solution)/shard_map/ppermute | solution.py:26
  201.0 8.4 %collective-permute-start.7 = (bf16[16,8192]{1,0:T(8,128)(2,1)S(1)}, bf16[16,8192]{1,0:T(8,128)(2,1)S(1)}, u32[]{:S(2)}, u32[]{:S(2)}) collective-permute-start(bf16[16,8192]{1,0:T(8,128)(2,1)S(1)} %get-tuple-element.52), channel_id=1, source_target_pairs={{0,4},{4,8},{8,12},{12,16},{16,20},{20,24},{24,28},{28,32},{32,36}... | collective-permute-start | bytes 786440 | tf_op jit(solution)/shard_map/ppermute | solution.py:26
  (7 other events, 53.0 us)
Sparse Core Ops, SparseCore 0:
  211.9 75.0 all-gather.1
where the time goes:
time: 572 us; the launch traced here: 567 us
  blocking collectives  251 us (44%)
  matrix products  122 us (21%)
  waiting for transfers between devices  81.5 us (14%)
  local copies, waits for them, and re-layouts  37.1 us (6%)
  other arithmetic  33.2 us (6%)
  starting transfers between devices  27 us (5%)
  between operations  15.2 us (3%)
    psum x1, blocking collectives, per_device(): intersection = lax.psum(partial_intersection, 'node') / total_nodes  251 us
    dot_general x8, matrix products, cell_terms(): jnp.einsum('sjk,jkn->skn', mixed, picker.astype(jnp.float32), precision=l...  82.7 us
    all_gather x1, waiting for transfers between devices, per_device(): panel = lax.all_gather(second, 'state', axis=0, tiled=True)  75.3 us
    dot_general x8, matrix products, cell_terms(): jnp.einsum('skn,jkn->sjk', part_pair, picker_half, preferred_element_type...  27.9 us
    ppermute x4, starting transfers between devices, passed_along(): return lax.ppermute(block, axis, route)  16.9 us
  transfers between devices with their start and end apart: 9, of which 4 were waited for; matrix products, arithmetic and copies ran while one was open for 1% of the time, Pallas kernels for 0%

commit v1 on v0

--- a/solution.py
+++ b/solution.py
@@ -101,7 +101,16 @@
         jnp.bfloat16
     )
     total_nodes = block.shape[1] * lax.axis_size("node")
-    panel = lax.all_gather(second, "state", axis=0, tiled=True)
+    ways = lax.axis_size("state")
+    up = [(d, (d + 1) % ways) for d in range(ways)]
+    down = [(d, (d - 1) % ways) for d in range(ways)]
+    earlier, later = ([second], [second])
+    for _ in range(ways // 2):
+        earlier.append(lax.ppermute(earlier[-1], "state", up))
+    for _ in range((ways - 1) // 2):
+        later.append(lax.ppermute(later[-1], "state", down))
+    line = jnp.concatenate([*earlier[::-1], *later[1:]], axis=0)
+    panel = jnp.roll(line, (lax.axis_index("state") - ways // 2) * second.shape[0], axis=0)
     partial_intersection = jnp.einsum("an,bn->ab", panel, panel, preferred_element_type=jnp.float32)
     intersection = lax.psum(partial_intersection, "node") / total_nodes
     factor, inverse = factorize(intersection)

time: 572 us -> 546 us (0.955)
  the two profiles are of different devices: /device:TPU:2 before, /device:TPU:128 now
where the time goes in v1:
time: 546 us; the launch traced here: 541 us
  blocking collectives  247 us (45%)
  matrix products  118 us (22%)
  waiting for transfers between devices  58.3 us (11%)
  local copies, waits for them, and re-layouts  42.9 us (8%)
  starting transfers between devices  40.7 us (7%)
  other arithmetic  32.2 us (6%)
    psum x1, blocking collectives, per_device(): intersection = lax.psum(partial_intersection, 'node') / total_nodes  247 us
    dot_general x8, matrix products, cell_terms(): jnp.einsum('sjk,jkn->skn', mixed, picker.astype(jnp.float32), precision=l...  82.7 us
    ppermute x2, waiting for transfers between devices, per_device(): earlier.append(lax.ppermute(earlier[-1], 'state', up))  36.4 us
    dot_general x8, matrix products, cell_terms(): jnp.einsum('skn,jkn->sjk', part_pair, picker_half, preferred_element_type...  27.9 us
    ppermute x4, starting transfers between devices, passed_along(): return lax.ppermute(block, axis, route)  18.2 us
    ppermute x4, waiting for transfers between devices, passed_along(): return lax.ppermute(block, axis, route)  18 us
    ppermute x2, starting transfers between devices, extended(): lax.ppermute(lax.slice_in_dim(block, 0, width, axis=dim), axis, backward)  13.9 us
  transfers between devices with their start and end apart: 11, of which 8 were waited for; matrix products, arithmetic and copies ran while one was open for 1% of the time, Pallas kernels for 0%

profile of v1, /device:TPU:128, one launch (start us, length us, event | category | flops | bytes accessed | tf_op | source)
XLA Modules:
  0.0 541.0 jit_solution(15764987307008870255)
XLA Ops:
  3.7 7.0 %collective-permute-start.1 = (bf16[16,8192]{1,0:T(8,128)(2,1)S(1)}, bf16[16,8192]{1,0:T(8,128)(2,1)S(1)}, u32[]{:S(2)}, u32[]{:S(2)}) collective-permute-start(bf16[16,8192]{1,0:T(8,128)(2,1)S(1)} %get-tuple-element.59), channel_id=1, source_target_pairs={{4,0},{8,4},{12,8},{16,12},{20,16},{24,20},{28,24},{32,28},{36,32}... | collective-permute-start | bytes 786440 | tf_op jit(solution)/shard_map/ppermute | solution.py:18
  29.7 4.3 fusion.126
  34.8 4.3 fusion.125
  41.0 4.2 fusion.124
  47.0 11.6 %fusion.45 = f32[16,128,192]{2,0,1:T(8,128)S(1)} fusion(s32[125,128]{0,1:T(8,128)S(1)} %copy.16, f32[16,128,125]{2,0,1:T(8,128)S(1)} %copy.33, f32[16,125,128]{1,0,2:T(8,128)} %get-tuple-element.75, f32[125,128]{0,1:T(8,128)} %copy.19), kind=kOutput, calls=%fused_computation.62 | convolution fusion | flops 593408000 | bytes 3748864 | tf_op jit(solution)/shard_map/sjk,jkn->skn/dot_general | solution.py:58
  58.6 9.9 %fusion.47 = f32[16,128,192]{2,0,1:T(8,128)S(1)} fusion(s32[125,128]{0,1:T(8,128)S(1)} %copy-done.12, f32[16,128,125]{2,0,1:T(8,128)S(1)} %copy.35, f32[16,125,128]{1,0,2:T(8,128)S(1)} %copy-done.20, f32[125,128]{0,1:T(8,128)S(1)} %copy-done.15), kind=kOutput, calls=%fused_computation.64 | convolution fusion | flops 593408000 | bytes 3748864 | tf_op jit(solution)/shard_map/sjk,jkn->skn/dot_general | solution.py:58
  68.5 10.0 %fusion.49 = f32[16,128,192]{2,0,1:T(8,128)S(1)} fusion(s32[125,128]{0,1:T(8,128)S(1)} %copy.22, f32[16,128,125]{2,0,1:T(8,128)S(1)} %copy-done.8, f32[16,125,128]{1,0,2:T(8,128)S(1)} %copy-done.21, f32[125,128]{0,1:T(8,128)S(1)} %copy.23), kind=kOutput, calls=%fused_computation.66 | convolution fusion | flops 593408000 | bytes 3748864 | tf_op jit(solution)/shard_map/sjk,jkn->skn/dot_general | solution.py:58
  78.5 9.8 %fusion.51 = f32[16,128,192]{2,0,1:T(8,128)S(1)} fusion(s32[125,128]{0,1:T(8,128)S(1)} %copy.24, f32[16,128,125]{2,0,1:T(8,128)S(1)} %copy-done.10, f32[16,125,128]{1,0,2:T(8,128)S(1)} %copy-done.22, f32[125,128]{0,1:T(8,128)S(1)} %copy.25), kind=kOutput, calls=%fused_computation.68 | convolution fusion | flops 593408000 | bytes 3748864 | tf_op jit(solution)/shard_map/sjk,jkn->skn/dot_general | solution.py:58
  94.9 4.0 reshape.133
  99.2 7.1 %collective-permute-start.2 = (bf16[16,8192]{1,0:T(8,128)(2,1)S(1)}, bf16[16,8192]{1,0:T(8,128)(2,1)S(1)}, u32[]{:S(2)}, u32[]{:S(2)}) collective-permute-start(bf16[16,8192]{1,0:T(8,128)(2,1)S(1)} %get-tuple-element.55), channel_id=1, source_target_pairs={{4,0},{8,4},{12,8},{16,12},{20,16},{24,20},{28,24},{32,28},{36,32}... | collective-permute-start | bytes 786440 | tf_op jit(solution)/shard_map/ppermute | solution.py:26
  110.2 7.9 %collective-permute-done.3 = bf16[16,8192]{1,0:T(8,128)(2,1)S(1)} collective-permute-done((bf16[16,8192]{1,0:T(8,128)(2,1)S(1)}, bf16[16,8192]{1,0:T(8,128)(2,1)S(1)}, u32[]{:S(2)}, u32[]{:S(2)}) %collective-permute-start.3) | collective-permute-done | bytes 262176 | tf_op jit(solution)/shard_map/ppermute | solution.py:26
  121.2 7.0 %collective-permute-start.5 = (bf16[16,8192]{1,0:T(8,128)(2,1)S(1)}, bf16[16,8192]{1,0:T(8,128)(2,1)S(1)}, u32[]{:S(2)}, u32[]{:S(2)}) collective-permute-start(bf16[16,8192]{1,0:T(8,128)(2,1)S(1)} %get-tuple-element.57), channel_id=1, source_target_pairs={{4,0},{8,4},{12,8},{16,12},{20,16},{24,20},{28,24},{32,28},{36,32}... | collective-permute-start | bytes 786440 | tf_op jit(solution)/shard_map/ppermute | solution.py:18
  158.7 11.7 %fusion.46 = f32[16,128,192]{2,0,1:T(8,128)S(1)} fusion(s32[125,128]{0,1:T(8,128)S(1)} %copy.16, f32[16,128,125]{2,0,1:T(8,128)} %copy.41, f32[16,125,128]{1,0,2:T(8,128)} %get-tuple-element.83, f32[125,128]{0,1:T(8,128)} %copy.19), kind=kOutput, calls=%fused_computation.63 | convolution fusion | flops 593408000 | bytes 3748864 | tf_op jit(solution)/shard_map/sjk,jkn->skn/dot_general | solution.py:58
  170.4 9.9 %fusion.48 = f32[16,128,192]{2,0,1:T(8,128)S(1)} fusion(s32[125,128]{0,1:T(8,128)S(1)} %copy-done.14, f32[16,128,125]{2,0,1:T(8,128)S(1)} %copy-done.9, f32[16,125,128]{1,0,2:T(8,128)S(1)} %copy-done.19, f32[125,128]{0,1:T(8,128)S(1)} %copy-done.16), kind=kOutput, calls=%fused_computation.65 | convolution fusion | flops 593408000 | bytes 3748864 | tf_op jit(solution)/shard_map/sjk,jkn->skn/dot_general | solution.py:58
  180.3 10.0 %fusion.50 = f32[16,128,192]{2,0,1:T(8,128)S(1)} fusion(s32[125,128]{0,1:T(8,128)S(1)} %copy.22, f32[16,128,125]{2,0,1:T(8,128)S(1)} %copy.45, f32[16,125,128]{1,0,2:T(8,128)S(1)} %copy-done.18, f32[125,128]{0,1:T(8,128)S(1)} %copy.23), kind=kOutput, calls=%fused_computation.67 | convolution fusion | flops 593408000 | bytes 3748864 | tf_op jit(solution)/shard_map/sjk,jkn->skn/dot_general | solution.py:58
  190.3 9.8 %fusion.52 = f32[16,128,192]{2,0,1:T(8,128)S(1)} fusion(s32[125,128]{0,1:T(8,128)S(1)} %copy.24, f32[16,128,125]{2,0,1:T(8,128)S(1)} %copy.47, f32[16,125,128]{1,0,2:T(8,128)S(1)} %copy-done.17, f32[125,128]{0,1:T(8,128)S(1)} %copy.25), kind=kOutput, calls=%fused_computation.69 | convolution fusion | flops 593408000 | bytes 3748864 | tf_op jit(solution)/shard_map/sjk,jkn->skn/dot_general | solution.py:58
  206.8 4.0 reshape.135
  211.1 7.3 %collective-permute-start.6 = (bf16[16,8192]{1,0:T(8,128)(2,1)S(1)}, bf16[16,8192]{1,0:T(8,128)(2,1)S(1)}, u32[]{:S(2)}, u32[]{:S(2)}) collective-permute-start(bf16[16,8192]{1,0:T(8,128)(2,1)S(1)} %get-tuple-element.53), channel_id=1, source_target_pairs={{4,0},{8,4},{12,8},{16,12},{20,16},{24,20},{28,24},{32,28},{36,32}... | collective-permute-start | bytes 786440 | tf_op jit(solution)/shard_map/ppermute | solution.py:26
  222.3 7.2 %collective-permute-done.7 = bf16[16,8192]{1,0:T(8,128)(2,1)S(1)} collective-permute-done((bf16[16,8192]{1,0:T(8,128)(2,1)S(1)}, bf16[16,8192]{1,0:T(8,128)(2,1)S(1)}, u32[]{:S(2)}, u32[]{:S(2)}) %collective-permute-start.7) | collective-permute-done | bytes 262176 | tf_op jit(solution)/shard_map/ppermute | solution.py:26
  232.4 21.8 %collective-permute-done.8 = bf16[16,32768]{1,0:T(8,128)(2,1)S(1)} collective-permute-done((bf16[16,32768]{1,0:T(8,128)(2,1)S(1)}, bf16[16,32768]{1,0:T(8,128)(2,1)S(1)}, u32[]{:S(2)}, u32[]{:S(2)}) %collective-permute-start.8) | collective-permute-done | bytes 1048608 | tf_op jit(solution)/shard_map/ppermute | solution.py:109
  257.4 14.6 %collective-permute-done.9 = bf16[16,32768]{1,0:T(8,128)(2,1)S(1)} collective-permute-done((bf16[16,32768]{1,0:T(8,128)(2,1)S(1)}, bf16[16,32768]{1,0:T(8,128)(2,1)S(1)}, u32[]{:S(2)}, u32[]{:S(2)}) %collective-permute-start.9) | collective-permute-done | bytes 1048608 | tf_op jit(solution)/shard_map/ppermute | solution.py:109
  277.2 246.6 %psum.7 = f32[64,64]{0,1:T(8,128)S(1)} all-reduce(f32[64,64]{0,1:T(8,128)S(1)} %fusion.39), channel_id=1, replica_groups=mesh['node'=64,'state'=4] {'node'}, use_global_device_ids=true, to_apply=%region_1.0 | all-reduce | flops 4096 | bytes 32768 | tf_op jit(solution)/shard_map/psum | solution.py:115
  523.8 5.8 %cholesky.17 = f32[64,64]{1,0:T(8,128)S(1)} custom-call(f32[64,64]{1,0:T(8,128)S(1)} %fusion.107), custom_call_target="Cholesky" | custom-call | tf_op jit(solution)/shard_map/jit(cholesky)/cholesky | solution.py:87
  531.6 4.9 custom-call.6
  (141 shorter events, 98.6 us)
Async XLA Ops:
  0.6 28.2 %copy-start = (bf16[125,125]{1,0:T(8,128)(2,1)S(1)}, bf16[125,125]{1,0:T(8,128)(2,1)}, u32[]{:S(2)}) copy-start(bf16[125,125]{1,0:T(8,128)(2,1)} %param.15) | copy-start | bytes 93754
  0.6 14.1 %copy-start.1 = (bf16[16,32768]{1,0:T(8,128)(2,1)S(1)}, bf16[16,32768]{1,0:T(8,128)(2,1)}, u32[]{:S(2)}) copy-start(bf16[16,32768]{1,0:T(8,128)(2,1)} %param.12) | copy-start | bytes 3145732
  1.8 12.9 %collective-permute-start = (bf16[16,8192]{1,0:T(8,128)(2,1)S(1)}, bf16[16,8192]{1,0:T(8,128)(2,1)S(1)}, u32[]{:S(2)}, u32[]{:S(2)}) collective-permute-start(bf16[16,8192]{1,0:T(8,128)(2,1)S(1)} %get-tuple-element.58), channel_id=1, source_target_pairs={{0,4},{4,8},{8,12},{12,16},{16,20},{20,24},{24,28},{28,32},{32,36}... | collective-permute-start | bytes 786440 | tf_op jit(solution)/shard_map/ppermute | solution.py:15
  3.7 11.0 %collective-permute-start.1 = (bf16[16,8192]{1,0:T(8,128)(2,1)S(1)}, bf16[16,8192]{1,0:T(8,128)(2,1)S(1)}, u32[]{:S(2)}, u32[]{:S(2)}) collective-permute-start(bf16[16,8192]{1,0:T(8,128)(2,1)S(1)} %get-tuple-element.59), channel_id=1, source_target_pairs={{4,0},{8,4},{12,8},{16,12},{20,16},{24,20},{28,24},{32,28},{36,32}... | collective-permute-start | bytes 786440 | tf_op jit(solution)/shard_map/ppermute | solution.py:18
  13.6 16.0 %copy-start.11 = (s32[125,128]{0,1:T(8,128)}, s32[125,128]{0,1:T(8,128)S(1)}, u32[]{:S(2)}) copy-start(s32[125,128]{0,1:T(8,128)S(1)} %copy.20) | copy-start | bytes 192004
  47.0 11.6 %copy-start.15 = (f32[125,128]{0,1:T(8,128)S(1)}, f32[125,128]{0,1:T(8,128)}, u32[]{:S(2)}) copy-start(f32[125,128]{0,1:T(8,128)} %copy.21) | copy-start | bytes 192004
  47.0 11.6 %copy-start.20 = (f32[16,125,128]{1,0,2:T(8,128)S(1)}, f32[16,125,128]{1,0,2:T(8,128)}, u32[]{:S(2)}) copy-start(f32[16,125,128]{1,0,2:T(8,128)} %get-tuple-element.73) | copy-start | bytes 3072004
  99.1 19.7 %copy-start.2 = (bf16[16,32768]{1,0:T(8,128)(2,1)S(1)}, bf16[16,32768]{1,0:T(8,128)(2,1)}, u32[]{:S(2)}) copy-start(bf16[16,32768]{1,0:T(8,128)(2,1)} %param.12) | copy-start | bytes 3145732
  99.2 10.9 %collective-permute-start.2 = (bf16[16,8192]{1,0:T(8,128)(2,1)S(1)}, bf16[16,8192]{1,0:T(8,128)(2,1)S(1)}, u32[]{:S(2)}, u32[]{:S(2)}) collective-permute-start(bf16[16,8192]{1,0:T(8,128)(2,1)S(1)} %get-tuple-element.55), channel_id=1, source_target_pairs={{4,0},{8,4},{12,8},{16,12},{20,16},{24,20},{28,24},{32,28},{36,32}... | collective-permute-start | bytes 786440 | tf_op jit(solution)/shard_map/ppermute | solution.py:26
  107.0 11.0 %collective-permute-start.3 = (bf16[16,8192]{1,0:T(8,128)(2,1)S(1)}, bf16[16,8192]{1,0:T(8,128)(2,1)S(1)}, u32[]{:S(2)}, u32[]{:S(2)}) collective-permute-start(bf16[16,8192]{1,0:T(8,128)(2,1)S(1)} %get-tuple-element.54), channel_id=1, source_target_pairs={{0,4},{4,8},{8,12},{12,16},{16,20},{20,24},{24,28},{28,32},{32,36}... | collective-permute-start | bytes 786440 | tf_op jit(solution)/shard_map/ppermute | solution.py:26
  119.2 12.8 %copy-start.4 = (bf16[16,32768]{1,0:T(8,128)(2,1)}, bf16[16,32768]{1,0:T(8,128)(2,1)S(1)}, u32[]{:S(2)}) copy-start(bf16[16,32768]{1,0:T(8,128)(2,1)S(1)} %fusion.43) | copy-start | bytes 3145732
  119.2 11.0 %collective-permute-start.4 = (bf16[16,8192]{1,0:T(8,128)(2,1)S(1)}, bf16[16,8192]{1,0:T(8,128)(2,1)S(1)}, u32[]{:S(2)}, u32[]{:S(2)}) collective-permute-start(bf16[16,8192]{1,0:T(8,128)(2,1)S(1)} %get-tuple-element.56), channel_id=1, source_target_pairs={{0,4},{4,8},{8,12},{12,16},{16,20},{20,24},{24,28},{28,32},{32,36}... | collective-permute-start | bytes 786440 | tf_op jit(solution)/shard_map/ppermute | solution.py:15
  121.2 10.8 %collective-permute-start.5 = (bf16[16,8192]{1,0:T(8,128)(2,1)S(1)}, bf16[16,8192]{1,0:T(8,128)(2,1)S(1)}, u32[]{:S(2)}, u32[]{:S(2)}) collective-permute-start(bf16[16,8192]{1,0:T(8,128)(2,1)S(1)} %get-tuple-element.57), channel_id=1, source_target_pairs={{4,0},{8,4},{12,8},{16,12},{20,16},{24,20},{28,24},{32,28},{36,32}... | collective-permute-start | bytes 786440 | tf_op jit(solution)/shard_map/ppermute | solution.py:18
  158.6 11.8 %copy-start.9 = (f32[16,128,125]{2,0,1:T(8,128)S(1)}, f32[16,128,125]{2,0,1:T(8,128)}, u32[]{:S(2)}) copy-start(f32[16,128,125]{2,0,1:T(8,128)} %copy.43) | copy-start | bytes 3072004
  158.6 11.8 %copy-start.14 = (s32[125,128]{0,1:T(8,128)S(1)}, s32[125,128]{0,1:T(8,128)}, u32[]{:S(2)}) copy-start(s32[125,128]{0,1:T(8,128)} %copy-done.11) | copy-start | bytes 192004
  158.6 11.8 %copy-start.16 = (f32[125,128]{0,1:T(8,128)S(1)}, f32[125,128]{0,1:T(8,128)}, u32[]{:S(2)}) copy-start(f32[125,128]{0,1:T(8,128)} %copy.21) | copy-start | bytes 192004
  158.6 11.8 %copy-start.19 = (f32[16,125,128]{1,0,2:T(8,128)S(1)}, f32[16,125,128]{1,0,2:T(8,128)}, u32[]{:S(2)}) copy-start(f32[16,125,128]{1,0,2:T(8,128)} %get-tuple-element.81) | copy-start | bytes 3072004
  211.0 19.3 %copy-start.3 = (bf16[16,32768]{1,0:T(8,128)(2,1)S(1)}, bf16[16,32768]{1,0:T(8,128)(2,1)}, u32[]{:S(2)}) copy-start(bf16[16,32768]{1,0:T(8,128)(2,1)} %param.12) | copy-start | bytes 3145732
  211.0 19.3 %copy-start.5 = (bf16[16,32768]{1,0:T(8,128)(2,1)S(1)}, bf16[16,32768]{1,0:T(8,128)(2,1)}, u32[]{:S(2)}) copy-start(bf16[16,32768]{1,0:T(8,128)(2,1)} %copy-done.4) | copy-start | bytes 3145732
  211.1 11.1 %collective-permute-start.6 = (bf16[16,8192]{1,0:T(8,128)(2,1)S(1)}, bf16[16,8192]{1,0:T(8,128)(2,1)S(1)}, u32[]{:S(2)}, u32[]{:S(2)}) collective-permute-start(bf16[16,8192]{1,0:T(8,128)(2,1)S(1)} %get-tuple-element.53), channel_id=1, source_target_pairs={{4,0},{8,4},{12,8},{16,12},{20,16},{24,20},{28,24},{32,28},{36,32}... | collective-permute-start | bytes 786440 | tf_op jit(solution)/shard_map/ppermute | solution.py:26
  218.5 11.0 %collective-permute-start.7 = (bf16[16,8192]{1,0:T(8,128)(2,1)S(1)}, bf16[16,8192]{1,0:T(8,128)(2,1)S(1)}, u32[]{:S(2)}, u32[]{:S(2)}) collective-permute-start(bf16[16,8192]{1,0:T(8,128)(2,1)S(1)} %get-tuple-element.52), channel_id=1, source_target_pairs={{0,4},{4,8},{8,12},{12,16},{16,20},{20,24},{24,28},{28,32},{32,36}... | collective-permute-start | bytes 786440 | tf_op jit(solution)/shard_map/ppermute | solution.py:26
  230.8 23.4 %collective-permute-start.8 = (bf16[16,32768]{1,0:T(8,128)(2,1)S(1)}, bf16[16,32768]{1,0:T(8,128)(2,1)S(1)}, u32[]{:S(2)}, u32[]{:S(2)}) collective-permute-start(bf16[16,32768]{1,0:T(8,128)(2,1)S(1)} %fusion.44), channel_id=1, source_target_pairs={{0,1},{1,2},{2,3},{3,0},{4,5},{5,6},{6,7},{7,4},{8,9},{9,10},{10,1... | collective-permute-start | bytes 3145736 | tf_op jit(solution)/shard_map/ppermute | solution.py:109
  254.2 17.9 %collective-permute-start.9 = (bf16[16,32768]{1,0:T(8,128)(2,1)S(1)}, bf16[16,32768]{1,0:T(8,128)(2,1)S(1)}, u32[]{:S(2)}, u32[]{:S(2)}) collective-permute-start(bf16[16,32768]{1,0:T(8,128)(2,1)S(1)} %collective-permute-done.8), channel_id=1, source_target_pairs={{0,1},{1,2},{2,3},{3,0},{4,5},{5,6},{6,7},{7,4},{8,9},{9,10},{10,1... | collective-permute-start | bytes 3145736 | tf_op jit(solution)/shard_map/ppermute | solution.py:109
  255.7 16.6 %collective-permute-start.10 = (bf16[16,32768]{1,0:T(8,128)(2,1)S(1)}, bf16[16,32768]{1,0:T(8,128)(2,1)S(1)}, u32[]{:S(2)}, u32[]{:S(2)}) collective-permute-start(bf16[16,32768]{1,0:T(8,128)(2,1)S(1)} %fusion.44), channel_id=1, source_target_pairs={{0,3},{1,0},{2,1},{3,2},{4,7},{5,4},{6,5},{7,6},{8,11},{9,8},{10,9... | collective-permute-start | bytes 3145736 | tf_op jit(solution)/shard_map/ppermute | solution.py:111
  (10 other events, 79.8 us)
